TPU v7x, 32 devices: a whole 2x2x4 slice. The times are simulated.
32 devices in a mesh: groups: 2 (over y), dp: 4 (over z), tensor: 4 (over x, core).
Axes of the slice: x: 2, y: 2, z: 4, core: 2. Of those that a mesh axis runs over, the one named last changes fastest.
Arguments:
- feature_cache: bfloat16 [512, 8, 3, 8192], P(('groups', 'dp'), None, None, 'tensor'), parts along dimension 0
- owner_ids: int32 [512, 1], P(('groups', 'dp')), parts along dimension 0, may hold values from 0 to 3; in each aligned block of 64 rows (0 to 63, 64 to 127, ...) at most 24 rows name the same one
- slot_ids: int32 [512], P(('groups', 'dp')), parts along dimension 0, may hold values from 0 to 63
- live_tokens: int32 [512], P(('groups', 'dp')), parts along dimension 0, may hold values from 1 to 8
- tap_gain: float32 [3, 8192], P(None, 'tensor'), may hold values from 0.1 to 1.9
- key_cotangent: bfloat16 [4096, 1024], P(('groups', 'dp'), 'tensor'), parts along dimension 0, may hold values from -0.1875 to 0.1875
- value_cotangent: bfloat16 [4096, 1024], P(('groups', 'dp'), 'tensor'), parts along dimension 0, may hold values from -0.1875 to 0.1875
Outputs:
- kv_gradient: float32 [4096, 8192], P(('groups', 'dp'), 'tensor'), parts along dimension 0
There are 2 independent parts, one for each index of `groups`. A program takes and returns all parts, laid end to end along the dimension named above; an argument that names none is the same for every part. Nothing has to cross between parts.
Inputs may be any that keep to these rules, and one draw needn't show every extreme that they name: `owner_ids`: among the 64 entries of one device's list, no owner is named more than 24 times, a bound that some block reaches.
All inputs are finite; a program needn't handle non-finite values.
Results may differ from a plain program's by a relative error of at most 0.009.
Values may be sent and summed in bfloat16 or wider, within the bound.
A program may use at most 128 MiB of HBM per device.

v0:
```python
import jax
import jax.numpy as jnp
from jax import lax
from jax.sharding import PartitionSpec as P

EPSILON = 1e-06


def united_of(feature_cache, tap_gain, width):
    floats = feature_cache.astype(jnp.float32)
    squares = lax.psum(jnp.sum(floats * floats, axis=-1), "tensor")
    inverse_rms = lax.rsqrt(squares / width + EPSILON)
    return jnp.sum(floats * inverse_rms[..., None] * tap_gain, axis=2).astype(jnp.bfloat16)


def slot_matrix(owner_ids, slot_ids, live_tokens, owned, dtype):
    index = owner_ids[:, 0] * owned + slot_ids
    table = lax.all_gather(jnp.stack([index, live_tokens]), "dp", axis=1, tiled=True)
    slots = lax.axis_size("dp") * owned
    chosen = jnp.arange(slots, dtype=jnp.int32)[:, None] == table[0][None, :]
    return (chosen.astype(dtype), table[1])


def body(feature_cache, owner_ids, slot_ids, live_tokens, tap_gain, key_cotangent, value_cotangent):
    owned, block_len, _, columns = feature_cache.shape
    width = columns * lax.axis_size("tensor")
    united = united_of(feature_cache, tap_gain, width).reshape(owned * block_len, columns)
    everywhere = lax.all_gather(united, "dp", axis=0, tiled=True)
    chosen, live = slot_matrix(owner_ids, slot_ids, live_tokens, owned, jnp.bfloat16)
    joined = jnp.concatenate(
        [
            lax.all_gather(key_cotangent, "tensor", axis=1, tiled=True),
            lax.all_gather(value_cotangent, "tensor", axis=1, tiled=True),
        ],
        axis=1,
    )
    mine = lax.all_to_all(joined, "dp", split_axis=1, concat_axis=0, tiled=True)
    rows = mine.shape[1]
    mine = mine.reshape(-1, block_len, rows)
    mask = jnp.arange(block_len, dtype=jnp.int32)[None, :] < live[:, None]
    mine = jnp.where(mask[:, :, None], mine, jnp.zeros_like(mine)).reshape(-1, block_len * rows)
    by_slot = (
        lax.dot_general(chosen, mine, (((1,), (0,)), ((), ())), preferred_element_type=jnp.float32)
        .astype(jnp.bfloat16)
        .reshape(-1, rows)
    )
    return lax.dot_general(
        by_slot, everywhere, (((0,), (0,)), ((), ())), preferred_element_type=jnp.float32
    )


def solution(mesh):
    in_specs = (
        P(("groups", "dp"), None, None, "tensor"),
        P(("groups", "dp"), None),
        P(("groups", "dp")),
        P(("groups", "dp")),
        P(None, "tensor"),
        P(("groups", "dp"), "tensor"),
        P(("groups", "dp"), "tensor"),
    )
    out_specs = P(("groups", "dp"), "tensor")
    return jax.shard_map(body, mesh=mesh, in_specs=in_specs, out_specs=out_specs, check_vma=False)
```

profile of v0, /device:TPU:0, one launch (start us, length us, event | category | flops | bytes accessed | tf_op | source)
XLA Modules:
  0.0 255.0 jit_solution(5300680193255701381)
XLA Ops:
  6.5 0.0 all-gather.5.cloned.1.call-start
  6.5 0.7 all-gather.5.cloned.1.call-update
  7.3 0.0 all-gather.7.cloned.1.call-start
  7.3 0.7 all-gather.7.cloned.1.call-update
  8.0 0.0 all-gather.9.cloned.1.call-start
  8.1 4.1 %fusion = f32[64,8,3]{1,2,0:T(4,128)S(1)} fusion(bf16[64,8,3,2048]{3,1,2,0:T(8,128)(2,1)} %param.7), kind=kLoop, calls=%fused_computation.2 | loop fusion | flops 9435648 | bytes 6297600 | tf_op jit(solution)/shard_map/reduce_sum | solution.py:11
  12.2 0.1 copy.17
  12.3 13.1 %psum.7 = f32[64,8,3]{0,1,2:T(8,128)S(1)} all-reduce(f32[64,8,3]{0,1,2:T(8,128)S(1)} %copy.17), channel_id=1, replica_groups=mesh['groups'=2,'dp'=4,'tensor'=4] {'tensor'}, use_global_device_ids=true, to_apply=%region_1.0 | all-reduce | flops 1536 | bytes 12288 | tf_op jit(solution)/shard_map/psum | solution.py:11
  25.4 0.1 copy.18
  25.5 0.0 copy-done
  25.5 6.9 %fusion.2 = bf16[64,8,2048]{2,1,0:T(8,128)(2,1)} fusion(bf16[64,8,3,2048]{3,1,2,0:T(8,128)(2,1)} %param.7, f32[3,2048]{1,0:T(4,128)S(1)} %copy-done, f32[64,8,3]{1,2,0:T(4,128)S(1)} %copy.18), kind=kLoop, calls=%fused_computation.4 | loop fusion | flops 11534336 | bytes 8419328 | tf_op jit(solution)/shard_map/reduce_sum | solution.py:13
  32.4 0.0 all-gather.9.cloned.1.call-update
  32.5 0.0 all-gather.5.cloned.1.call-done
  32.5 14.6 %all-gather.7.cloned.1.call-done = bf16[512,1024]{1,0:T(8,128)(2,1)} async-done(((bf16[512,256]{1,0:T(8,128)(2,1)}), bf16[512,1024]{1,0:T(8,128)(2,1)}) %all-gather.7.cloned.1.call-update) | async-done | bytes 1048592 | tf_op jit(solution)/shard_map/all_gather | solution.py:33
  47.0 1.7 pad_maximum_fusion
  48.8 0.0 copy-start.2
  48.8 0.0 copy-start.3
  48.8 0.0 copy-start.1
  48.8 1.5 copy.22
  50.3 4.6 %all-to-all-start = ((bf16[512,4,512]{2,0,1:T(8,128)(2,1)}), bf16[512,4,512]{2,0,1:T(8,128)(2,1)S(1)}, u32[]{:S(2)}, u32[]{:S(2)}) async-start(bf16[512,4,512]{2,0,1:T(8,128)(2,1)} %bitcast.29), calls=%async_computation | async-start | bytes 4194304 | tf_op jit(solution)/shard_map/all_to_all | solution.py:37
  54.9 0.0 copy-done.2
  55.0 71.3 %all-gather = s32[4,64,2]{1,2,0:T(2,128)S(1)} all-gather(s32[1,64,2]{1,2,0:T(2,128)S(1)} %add_bitcast_fusion), channel_id=1, replica_groups=mesh['groups'=2,'dp'=4,'tensor'=4] {'dp'}, dimensions={0}, use_global_device_ids=true | all-gather | bytes 2560 | tf_op jit(solution)/shard_map/all_gather | solution.py:18
  126.3 0.1 reshape.47
  126.4 0.1 iota_compare_fusion.2
  126.5 0.5 broadcast_in_dim.18
  126.9 0.8 copy.20
  127.7 32.2 %all-to-all-done = bf16[512,4,512]{2,0,1:T(8,128)(2,1)S(1)} async-done(((bf16[512,4,512]{2,0,1:T(8,128)(2,1)}), bf16[512,4,512]{2,0,1:T(8,128)(2,1)S(1)}, u32[]{:S(2)}, u32[]{:S(2)}) %all-to-all-start) | async-done | bytes 2097184 | tf_op jit(solution)/shard_map/all_to_all | solution.py:37
  159.9 2.3 reshape.44
  162.3 3.7 %convolution_convert_fusion = bf16[256,4096]{1,0:T(8,128)(2,1)} fusion(pred[256,4096]{1,0:T(8,128)(4,1)S(1)} %bitcast.33, bf16[256,4096]{1,0:T(8,128)(2,1)} %reshape.44, s32[256]{0:T(256)S(1)} %bitcast.36), kind=kOutput, calls=%fused_computation.5 | convolution fusion | flops 539033600 | bytes 5243904 | tf_op jit(solution)/shard_map/dot_general | solution.py:43
  165.9 2.9 %reshape.45 = bf16[2048,512]{1,0:T(8,128)(2,1)S(1)} reshape(bf16[256,4096]{1,0:T(8,128)(2,1)} %convolution_convert_fusion) | data formatting | bytes 4194304 | tf_op jit(solution)/shard_map/reshape | solution.py:45
  168.8 70.2 %all-gather.9.cloned.1.call-done = bf16[2048,2048]{1,0:T(8,128)(2,1)} async-done(((bf16[512,2048]{1,0:T(8,128)(2,1)}), bf16[2048,2048]{1,0:T(8,128)(2,1)}) %all-gather.9.cloned.1.call-update) | async-done | bytes 8388624 | tf_op jit(solution)/shard_map/all_gather | solution.py:28
  239.0 9.4 %fusion.9 = f32[512,2048]{1,0:T(8,128)} fusion(bf16[2048,512]{1,0:T(8,128)(2,1)S(1)} %reshape.45, bf16[2048,2048]{1,0:T(8,128)(2,1)} %all-gather.9.cloned.1.call-done), kind=kOutput, calls=%fused_computation.20 | convolution fusion | flops 4294967296 | bytes 14680064 | tf_op jit(solution)/shard_map/dot_general | solution.py:47
  (8 shorter events, 0.0 us)
Async XLA Ops:
  6.5 19.0 %copy-start = (f32[3,2048]{1,0:T(4,128)S(1)}, f32[3,2048]{1,0:T(4,128)}, u32[]{:S(2)}) copy-start(f32[3,2048]{1,0:T(4,128)} %param.11) | copy-start | bytes 73732
  6.5 25.9 %all-gather.5.cloned.1.call-start = ((), (), s32[]{:S(2)}) async-start(), calls=%async_computation.1 | async-start | bytes 1310720 | tf_op jit(solution)/shard_map/all_gather | solution.py:32
  7.3 39.8 %all-gather.7.cloned.1.call-start = ((), (), s32[]{:S(2)}) async-start(), calls=%async_computation.2 | async-start | bytes 1310720 | tf_op jit(solution)/shard_map/all_gather | solution.py:33
  8.0 231.0 %all-gather.9.cloned.1.call-start = ((), (), s32[]{:S(2)}) async-start(), calls=%async_computation.3 | async-start | bytes 10485760 | tf_op jit(solution)/shard_map/all_gather | solution.py:28
  48.8 6.1 %copy-start.2 = (s32[64]{0:T(128)S(1)}, s32[64]{0:T(128)}, u32[]{:S(2)}) copy-start(s32[64]{0:T(128)} %param.9) | copy-start | bytes 772
  48.8 6.1 %copy-start.3 = (s32[64,1]{0,1:T(1,128)S(1)}, s32[64,1]{0,1:T(1,128)}, u32[]{:S(2)}) copy-start(s32[64,1]{0,1:T(1,128)} %param.8) | copy-start | bytes 772
  48.8 6.1 %copy-start.1 = (s32[64]{0:T(128)S(1)}, s32[64]{0:T(128)}, u32[]{:S(2)}) copy-start(s32[64]{0:T(128)} %param.10) | copy-start | bytes 772
  50.3 109.6 %all-to-all-start = ((bf16[512,4,512]{2,0,1:T(8,128)(2,1)}), bf16[512,4,512]{2,0,1:T(8,128)(2,1)S(1)}, u32[]{:S(2)}, u32[]{:S(2)}) async-start(bf16[512,4,512]{2,0,1:T(8,128)(2,1)} %bitcast.29), calls=%async_computation | async-start | bytes 4194304 | tf_op jit(solution)/shard_map/all_to_all | solution.py:37
Sparse Core Ops, SparseCore 0:
  8.9 19.6 all-gather.4
  30.2 16.8 all-gather.6
  48.6 190.3 all-gather.8
where the time goes:
time: 255 us
  waiting for transfers between devices  118 us (46%)
  blocking collectives  84.5 us (33%)
  between operations  13.2 us (5%)
  matrix products  13.1 us (5%)
  other arithmetic  12.9 us (5%)
  local copies, waits for them, and re-layouts  8.19 us (3%)
  starting transfers between devices  4.68 us (2%)
    all_gather x1, blocking collectives, slot_matrix(): lax.all_gather(jnp.stack([index, live_tokens]), 'dp', axis=1, tiled=True)  71.3 us
    all_gather x1, waiting for transfers between devices, body(): everywhere = lax.all_gather(united, 'dp', axis=0, tiled=True)  70.2 us
    all_to_all x1, waiting for transfers between devices, body(): mine = lax.all_to_all(joined, 'dp', split_axis=1, concat_axis=0, tiled=True)  32.2 us
    all_gather x1, waiting for transfers between devices, body(): lax.all_gather(value_cotangent, 'tensor', axis=1, tiled=True)  14.6 us
    psum x1, blocking collectives, united_of(): squares = lax.psum(jnp.sum(floats * floats, axis=-1), 'tensor')  13.1 us
    dot_general x1, matrix products, body(): lax.dot_general(by_slot, everywhere, (((0,), (0,)), ((), ())), preferred_...  9.44 us
    reduce_sum x1, other arithmetic, united_of(): jnp.sum(floats * inverse_rms[..., None] * tap_gain, axis=2)  6.9 us
  transfers between devices with their start and end apart: 4, of which 3 were waited for; matrix products, arithmetic and copies ran while one was open for 10% of the time, Pallas kernels for 0%

commit v1 on v0

--- a/solution.py
+++ b/solution.py
@@ -22,6 +22,20 @@
 
 
 def body(feature_cache, owner_ids, slot_ids, live_tokens, tap_gain, key_cotangent, value_cotangent):
+
+    def make_the_bands(load):
+        wide_out, r1 = (jax.lax.psum(1, "tensor"), jax.lax.axis_index("tensor"))
+        f_next, left_arr = (load, 1)
+        while left_arr < wide_out:
+            outcome_arr = jax.lax.ppermute(
+                f_next, "tensor", [(dev_j, dev_j ^ left_arr) for dev_j in range(wide_out)]
+            )
+            high = jnp.concatenate([f_next, outcome_arr], axis=1)
+            mixed_arr = jnp.concatenate([outcome_arr, f_next], axis=1)
+            f_next = jnp.where(r1 & left_arr == 0, high, mixed_arr)
+            left_arr = 2 * left_arr
+        return f_next
+
     owned, block_len, _, columns = feature_cache.shape
     width = columns * lax.axis_size("tensor")
     united = united_of(feature_cache, tap_gain, width).reshape(owned * block_len, columns)
@@ -30,7 +44,7 @@
     joined = jnp.concatenate(
         [
             lax.all_gather(key_cotangent, "tensor", axis=1, tiled=True),
-            lax.all_gather(value_cotangent, "tensor", axis=1, tiled=True),
+            make_the_bands(value_cotangent),
         ],
         axis=1,
     )

time: 255 us -> 243 us (0.953)
  waiting for transfers between devices: 118 us -> 101 us
  blocking collectives: 84.5 us -> 87.1 us
    ppermute x0 -> x2, waiting for transfers between devices: none -> 15.1 us  [make_the_bands(): jax.lax.ppermute(f_next, 'tensor', [(dev_j, dev_j ^ left_arr) for dev_j i...]
    all_gather x1 -> x0, waiting for transfers between devices: 14.6 us -> none  [body(): lax.all_gather(value_cotangent, 'tensor', axis=1, tiled=True)]
    all_gather x1, waiting for transfers between devices: 70.2 us -> 58.7 us  [body(): everywhere = lax.all_gather(united, 'dp', axis=0, tiled=True)]
    all_to_all x1, waiting for transfers between devices: 32.2 us -> 27 us  [body(): mine = lax.all_to_all(joined, 'dp', split_axis=1, concat_axis=0, tiled=True)]
    all_gather x1, blocking collectives: 71.3 us -> 74 us  [slot_matrix(): lax.all_gather(jnp.stack([index, live_tokens]), 'dp', axis=1, tiled=True)]
  transfers between devices with their start and end apart: 4 -> 5, of which waited for: 3 -> 4; matrix products, arithmetic and copies ran while one was open for 10% -> 10% of each run, Pallas kernels for 0% -> 0%
where the time goes in v1:
time: 243 us
  waiting for transfers between devices  101 us (42%)
  blocking collectives  87.1 us (36%)
  between operations  13.5 us (6%)
  matrix products  13.1 us (5%)
  other arithmetic  12.9 us (5%)
  local copies, waits for them, and re-layouts  9.11 us (4%)
  starting transfers between devices  5.49 us (2%)
    all_gather x1, blocking collectives, slot_matrix(): lax.all_gather(jnp.stack([index, live_tokens]), 'dp', axis=1, tiled=True)  74 us
    all_gather x1, waiting for transfers between devices, body(): everywhere = lax.all_gather(united, 'dp', axis=0, tiled=True)  58.7 us
    all_to_all x1, waiting for transfers between devices, body(): mine = lax.all_to_all(joined, 'dp', split_axis=1, concat_axis=0, tiled=True)  27 us
    ppermute x2, waiting for transfers between devices, make_the_bands(): jax.lax.ppermute(f_next, 'tensor', [(dev_j, dev_j ^ left_arr) for dev_j i...  15.1 us
    psum x1, blocking collectives, united_of(): squares = lax.psum(jnp.sum(floats * floats, axis=-1), 'tensor')  13.1 us
    dot_general x1, matrix products, body(): lax.dot_general(by_slot, everywhere, (((0,), (0,)), ((), ())), preferred_...  9.44 us
    reduce_sum x1, other arithmetic, united_of(): jnp.sum(floats * inverse_rms[..., None] * tap_gain, axis=2)  6.86 us
    all_to_all x1, starting transfers between devices, body(): mine = lax.all_to_all(joined, 'dp', split_axis=1, concat_axis=0, tiled=True)  4.97 us
  transfers between devices with their start and end apart: 5, of which 4 were waited for; matrix products, arithmetic and copies ran while one was open for 10% of the time, Pallas kernels for 0%

profile of v1, /device:TPU:0, one launch (start us, length us, event | category | flops | bytes accessed | tf_op | source)
XLA Modules:
  0.0 242.8 jit_solution(5431102361711027277)
XLA Ops:
  6.5 0.0 all-gather.4.cloned.1.call-start
  6.5 0.7 all-gather.4.cloned.1.call-update
  7.3 0.0 all-gather.6.cloned.1.call-start
  7.3 4.1 %fusion = f32[64,8,3]{1,2,0:T(4,128)S(1)} fusion(bf16[64,8,3,2048]{3,1,2,0:T(8,128)(2,1)} %param.7), kind=kLoop, calls=%fused_computation.2 | loop fusion | flops 9435648 | bytes 6297600 | tf_op jit(solution)/shard_map/reduce_sum | solution.py:11
  11.4 0.1 copy.17
  11.5 13.1 %psum.7 = f32[64,8,3]{0,1,2:T(8,128)S(1)} all-reduce(f32[64,8,3]{0,1,2:T(8,128)S(1)} %copy.17), channel_id=1, replica_groups=mesh['groups'=2,'dp'=4,'tensor'=4] {'tensor'}, use_global_device_ids=true, to_apply=%region_1.0 | all-reduce | flops 1536 | bytes 12288 | tf_op jit(solution)/shard_map/psum | solution.py:11
  24.6 0.1 copy.18
  24.8 6.9 %fusion.2 = bf16[64,8,2048]{2,1,0:T(8,128)(2,1)} fusion(bf16[64,8,3,2048]{3,1,2,0:T(8,128)(2,1)} %param.7, f32[3,2048]{1,0:T(4,128)S(1)} %copy-done.1, f32[64,8,3]{1,2,0:T(4,128)S(1)} %copy.18), kind=kLoop, calls=%fused_computation.4 | loop fusion | flops 11534336 | bytes 8419328 | tf_op jit(solution)/shard_map/reduce_sum | solution.py:13
  31.6 0.0 all-gather.6.cloned.1.call-update
  31.7 0.9 copy-done
  32.6 0.0 collective-permute-start
  32.6 1.5 collective-permute-done
  34.1 0.1 maximum_select_fusion.1
  34.2 0.5 collective-permute-start.1
  34.7 13.6 %collective-permute-done.1 = bf16[512,512]{1,0:T(8,128)(2,1)S(1)} collective-permute-done((bf16[512,512]{1,0:T(8,128)(2,1)S(1)}, bf16[512,512]{1,0:T(8,128)(2,1)S(1)}, u32[]{:S(2)}, u32[]{:S(2)}) %collective-permute-start.1) | collective-permute-done | bytes 524320 | tf_op jit(solution)/shard_map/ppermute | solution.py:30
  48.3 0.3 maximum_select_fusion
  48.6 0.0 all-gather.4.cloned.1.call-done
  48.6 1.4 pad_maximum_fusion
  50.0 1.5 copy.22
  51.5 5.0 %all-to-all-start = ((bf16[512,4,512]{2,0,1:T(8,128)(2,1)}), bf16[512,4,512]{2,0,1:T(8,128)(2,1)S(1)}, u32[]{:S(2)}, u32[]{:S(2)}) async-start(bf16[512,4,512]{2,0,1:T(8,128)(2,1)} %bitcast.29), calls=%async_computation | async-start | bytes 4194304 | tf_op jit(solution)/shard_map/all_to_all | solution.py:51
  56.5 0.0 copy-done.3
  56.5 74.0 %all-gather = s32[4,64,2]{1,2,0:T(2,128)S(1)} all-gather(s32[1,64,2]{1,2,0:T(2,128)S(1)} %add_bitcast_fusion), channel_id=1, replica_groups=mesh['groups'=2,'dp'=4,'tensor'=4] {'dp'}, dimensions={0}, use_global_device_ids=true | all-gather | bytes 2560 | tf_op jit(solution)/shard_map/all_gather | solution.py:18
  130.5 0.1 reshape.47
  130.6 0.1 iota_compare_fusion.2
  130.7 0.5 broadcast_in_dim.18
  131.2 0.8 copy.20
  131.9 27.0 %all-to-all-done = bf16[512,4,512]{2,0,1:T(8,128)(2,1)S(1)} async-done(((bf16[512,4,512]{2,0,1:T(8,128)(2,1)}), bf16[512,4,512]{2,0,1:T(8,128)(2,1)S(1)}, u32[]{:S(2)}, u32[]{:S(2)}) %all-to-all-start) | async-done | bytes 2097184 | tf_op jit(solution)/shard_map/all_to_all | solution.py:51
  158.9 2.3 reshape.44
  161.2 3.7 %convolution_convert_fusion = bf16[256,4096]{1,0:T(8,128)(2,1)} fusion(pred[256,4096]{1,0:T(8,128)(4,1)S(1)} %bitcast.33, bf16[256,4096]{1,0:T(8,128)(2,1)} %reshape.44, s32[256]{0:T(256)S(1)} %bitcast.36), kind=kOutput, calls=%fused_computation.5 | convolution fusion | flops 539033600 | bytes 5243904 | tf_op jit(solution)/shard_map/dot_general | solution.py:57
  164.9 2.9 %reshape.45 = bf16[2048,512]{1,0:T(8,128)(2,1)S(1)} reshape(bf16[256,4096]{1,0:T(8,128)(2,1)} %convolution_convert_fusion) | data formatting | bytes 4194304 | tf_op jit(solution)/shard_map/reshape | solution.py:59
  167.8 58.7 %all-gather.6.cloned.1.call-done = bf16[2048,2048]{1,0:T(8,128)(2,1)} async-done(((bf16[512,2048]{1,0:T(8,128)(2,1)}), bf16[2048,2048]{1,0:T(8,128)(2,1)}) %all-gather.6.cloned.1.call-update) | async-done | bytes 8388624 | tf_op jit(solution)/shard_map/all_gather | solution.py:42
  226.5 9.4 %fusion.9 = f32[512,2048]{1,0:T(8,128)} fusion(bf16[2048,512]{1,0:T(8,128)(2,1)S(1)} %reshape.45, bf16[2048,2048]{1,0:T(8,128)(2,1)} %all-gather.6.cloned.1.call-done), kind=kOutput, calls=%fused_computation.22 | convolution fusion | flops 4294967296 | bytes 14680064 | tf_op jit(solution)/shard_map/dot_general | solution.py:61
  (13 shorter events, 0.0 us)
Async XLA Ops:
  6.5 42.1 %all-gather.4.cloned.1.call-start = ((), (), s32[]{:S(2)}) async-start(), calls=%async_computation.1 | async-start | bytes 1310720 | tf_op jit(solution)/shard_map/all_gather | solution.py:46
  7.3 17.5 %copy-start.1 = (f32[3,2048]{1,0:T(4,128)S(1)}, f32[3,2048]{1,0:T(4,128)}, u32[]{:S(2)}) copy-start(f32[3,2048]{1,0:T(4,128)} %param.11) | copy-start | bytes 73732
  7.3 219.2 %all-gather.6.cloned.1.call-start = ((), (), s32[]{:S(2)}) async-start(), calls=%async_computation.2 | async-start | bytes 10485760 | tf_op jit(solution)/shard_map/all_gather | solution.py:42
  31.6 0.9 copy-start
  32.6 1.5 collective-permute-start
  34.2 14.0 %collective-permute-start.1 = (bf16[512,512]{1,0:T(8,128)(2,1)S(1)}, bf16[512,512]{1,0:T(8,128)(2,1)S(1)}, u32[]{:S(2)}, u32[]{:S(2)}) collective-permute-start(bf16[512,512]{1,0:T(8,128)(2,1)S(1)} %maximum_select_fusion.1), channel_id=1, source_target_pairs={{0,2},{1,3},{2,0},{3,1},{4,6},{5,7},{6,4},{7,5},{8,10},{9,11},{10,... | collective-permute-start | bytes 1572872 | tf_op jit(solution)/shard_map/ppermute | solution.py:30
  51.5 5.0 %copy-start.3 = (s32[64]{0:T(128)S(1)}, s32[64]{0:T(128)}, u32[]{:S(2)}) copy-start(s32[64]{0:T(128)} %param.9) | copy-start | bytes 772
  51.5 5.0 %copy-start.4 = (s32[64,1]{0,1:T(1,128)S(1)}, s32[64,1]{0,1:T(1,128)}, u32[]{:S(2)}) copy-start(s32[64,1]{0,1:T(1,128)} %param.8) | copy-start | bytes 772
  51.5 5.0 %copy-start.2 = (s32[64]{0:T(128)S(1)}, s32[64]{0:T(128)}, u32[]{:S(2)}) copy-start(s32[64]{0:T(128)} %param.10) | copy-start | bytes 772
  51.5 107.4 %all-to-all-start = ((bf16[512,4,512]{2,0,1:T(8,128)(2,1)}), bf16[512,4,512]{2,0,1:T(8,128)(2,1)S(1)}, u32[]{:S(2)}, u32[]{:S(2)}) async-start(bf16[512,4,512]{2,0,1:T(8,128)(2,1)} %bitcast.29), calls=%async_computation | async-start | bytes 4194304 | tf_op jit(solution)/shard_map/all_to_all | solution.py:51
Sparse Core Ops, SparseCore 0:
  8.9 19.6 all-gather.3
  31.8 194.6 all-gather.5
